TPU v7x, 512 devices: a whole 4x4x16 slice. The times are simulated.
512 devices in a mesh: dp: 32 (over x, z_lo, core), tensor: 16 (over z_hi, y).
Axes of the slice: x: 4, y: 4, z: 16 (z_hi: 4, z_lo: 4; z = z_hi * 4 + z_lo), core: 2. Of those that a mesh axis runs over, the one named last changes fastest.
Arguments:
- page_patches: bfloat16 [32768, 6144], P('dp', 'tensor'), may hold values from -720 to 720
- gain: bfloat16 [6144], P('tensor'), may hold values from 0.5 to 1.5
- q_weight: bfloat16 [6144, 4096], P('dp', 'tensor'), may hold values from -0.076546554 to 0.076546554
- k_weight: bfloat16 [6144, 4096], P('dp', 'tensor'), may hold values from -2.0412415 to 2.0412415
- v_weight: bfloat16 [6144, 4096], P('dp', 'tensor'), may hold values from -0.078125 to 0.078125
- pack_lengths: int32 [32, 32], replicated, may hold values from 1 to 32, 512 in all within a row
- line_order: int32 [32, 32], replicated, may hold values from 0 to 31, each once within a row
Outputs:
- context: bfloat16 [16384, 4096], P('dp', 'tensor')
Inputs may be any that keep to these rules, and one draw needn't show every extreme that they name: `pack_lengths`: every row sums to exactly 512 and holds the value 32. `line_order`: each row names every sequence 0 to 31 once.
All inputs are finite; a program needn't handle non-finite values.
Results may differ from a plain program's by a relative error of at most 0.0079.
Values may be sent and summed in bfloat16 or wider, within the bound.
No kernel may reach another device: no remote copies, remote signals or barrier semaphores. Data moves between devices by JAX's collectives and lax.ppermute only.
A program may use at most 64 MiB of HBM per device.

v0:
```python
import math
import jax
import jax.numpy as jnp
from jax import lax
from jax.sharding import PartitionSpec as P

HEAD_DIM = 128
norm_epsilon = 1e-06


def shards(page_patches, gain, q_weight, k_weight, v_weight, pack_lengths, line_order):
    groups = lax.axis_size("dp")
    page_index = lax.axis_index("dp")
    feature_cols = page_patches.shape[1]
    slot_rows = page_patches.shape[0] // groups
    seq_rows = slot_rows * groups // 2
    targets = jnp.arange(groups, dtype=jnp.int32)
    my_order = lax.dynamic_index_in_dim(line_order, page_index, 0, keepdims=False)
    slot_for = jnp.sum(
        jnp.where(my_order[None, :] == targets[:, None], targets[None, :], 0), axis=1
    )
    slots = page_patches.reshape(groups, slot_rows, feature_cols)
    outgoing = jnp.take(slots, slot_for, axis=0)
    incoming = lax.all_to_all(outgoing, "dp", split_axis=0, concat_axis=0, tiled=True)
    my_lengths = lax.dynamic_index_in_dim(pack_lengths, page_index, 0, keepdims=False)
    line_ends = jnp.cumsum(my_lengths)
    line_starts = line_ends - my_lengths
    places = jnp.arange(seq_rows, dtype=jnp.int32)
    segment = jnp.sum((line_ends[None, :] <= places[:, None]).astype(jnp.int32), axis=1)
    start_of_row = jnp.sum(
        jnp.where(segment[:, None] == targets[None, :], line_starts[None, :], 0), axis=1
    )
    source_rows = segment * slot_rows + places - start_of_row
    packed = jnp.take(incoming.reshape(groups * slot_rows, feature_cols), source_rows, axis=0)
    full_rows, full_gain = (
        lax.all_gather(packed, "tensor", axis=1, tiled=True),
        lax.all_gather(gain, "tensor", axis=0, tiled=True),
    )
    row_vals = full_rows.astype(jnp.float32)
    row_mean = jnp.mean(row_vals, axis=1, keepdims=True)
    row_var = jnp.mean(jnp.square(row_vals - row_mean), axis=1, keepdims=True)
    normed = (
        (row_vals - row_mean) * lax.rsqrt(row_var + norm_epsilon) * full_gain.astype(jnp.float32)
    ).astype(jnp.bfloat16)
    pieces = (
        lax.all_gather(q_weight, "dp", axis=0, tiled=True),
        lax.all_gather(k_weight, "dp", axis=0, tiled=True),
        lax.all_gather(v_weight, "dp", axis=0, tiled=True),
    )
    query_sum, key_sum, value_sum = tuple(
        (jnp.dot(normed, weight_rows, preferred_element_type=jnp.float32) for weight_rows in pieces)
    )
    local_heads = q_weight.shape[1] // HEAD_DIM
    query_heads = query_sum.astype(jnp.bfloat16).reshape(seq_rows, local_heads, HEAD_DIM)
    key_heads = key_sum.astype(jnp.bfloat16).reshape(seq_rows, local_heads, HEAD_DIM)
    value_heads = value_sum.astype(jnp.bfloat16).reshape(seq_rows, local_heads, HEAD_DIM)
    scores = jnp.einsum(
        "qhd,khd->hqk", query_heads, key_heads, preferred_element_type=jnp.float32
    ) * (1.0 / math.sqrt(HEAD_DIM))
    same_line = segment[:, None] == segment[None, :]
    scores = jnp.where(same_line[None, :, :], scores, -jnp.inf)
    row_max = jnp.max(scores, axis=2, keepdims=True)
    expo = jnp.exp(scores - row_max)
    attn_probs = (expo / jnp.sum(expo, axis=2, keepdims=True)).astype(jnp.bfloat16)
    context = jnp.einsum(
        "hqk,khd->qhd", attn_probs, value_heads, preferred_element_type=jnp.float32
    )
    return context.astype(jnp.bfloat16).reshape(seq_rows, local_heads * HEAD_DIM)


def solution(mesh):
    return jax.shard_map(
        shards,
        mesh=mesh,
        in_specs=(
            P("dp", "tensor"),
            P("tensor"),
            P("dp", "tensor"),
            P("dp", "tensor"),
            P("dp", "tensor"),
            P(),
            P(),
        ),
        out_specs=P("dp", "tensor"),
        check_vma=False,
    )
```

profile of v0, /device:TPU:1, one launch (start us, length us, event | category | flops | bytes accessed | tf_op | source)
XLA Modules:
  0.0 443.6 jit_solution(14901982915176972839)
XLA Ops:
  6.5 0.0 copy-start
  6.5 0.8 dynamic-slice_bitcast_fusion
  7.3 0.1 select_reduce_fusion.1
  7.5 0.2 copy-done
  7.7 0.7 gather_fusion
  8.4 1.0 broadcast_select_fusion
  9.4 0.0 copy-start.2
  9.4 10.6 %all-to-all-start = ((bf16[32,32,384]{2,1,0:T(8,128)(2,1)}), bf16[32,32,384]{2,1,0:T(8,128)(2,1)S(1)}, u32[]{:S(2)}, u32[]{:S(2)}) async-start(bf16[32,32,384]{2,1,0:T(8,128)(2,1)} %broadcast_select_fusion), calls=%async_computation | async-start | bytes 1572864 | tf_op jit(solution)/shard_map/all_to_all | solution.py:24
  20.0 0.0 all-gather.6.cloned.1.call-start
  20.1 0.7 fusion.17
  20.8 0.1 copy.23
  20.9 0.1 reduce-window.4
  20.9 0.1 reduce
  21.0 0.1 convert_reduce_fusion.1
  21.1 0.7 fusion.13
  21.8 0.1 select_reduce_fusion
  22.0 20.5 %all-to-all-done = bf16[32,32,384]{2,1,0:T(8,128)(2,1)S(1)} async-done(((bf16[32,32,384]{2,1,0:T(8,128)(2,1)}), bf16[32,32,384]{2,1,0:T(8,128)(2,1)S(1)}, u32[]{:S(2)}, u32[]{:S(2)}) %all-to-all-start) | async-done | bytes 786464 | tf_op jit(solution)/shard_map/all_to_all | solution.py:24
  42.5 1.9 gather_fusion.1
  44.4 0.9 broadcast_select_fusion.1
  45.3 0.0 all-gather.6.cloned.1.call-update
  45.3 0.0 all-gather.10.cloned.1.call-start
  45.4 0.7 all-gather.10.cloned.1.call-update
  46.1 0.0 all-gather.12.cloned.1.call-start
  46.1 0.7 all-gather.12.cloned.1.call-update
  46.8 0.0 all-gather.8.cloned.1.call-start
  46.9 0.5 all-gather.8.cloned.1.call-update
  47.4 0.0 copy-done.2
  47.4 49.9 %all-gather = bf16[16,1,384]{2,1,0:T(2,128)(2,1)S(1)} all-gather(bf16[1,1,384]{2,1,0:T(2,128)(2,1)S(1)} %reshape.150), channel_id=1, replica_groups=mesh['dp'=32,'tensor'=16] {'tensor'}, dimensions={0}, use_global_device_ids=true | all-gather | bytes 13056 | tf_op jit(solution)/shard_map/all_gather | solution.py:37
  97.4 0.2 broadcast_compare_fusion
  97.6 133.5 %all-gather.6.cloned.1.call-done = bf16[512,6144]{1,0:T(8,128)(2,1)} async-done(((bf16[512,384]{1,0:T(8,128)(2,1)}), bf16[512,6144]{1,0:T(8,128)(2,1)}) %all-gather.6.cloned.1.call-update) | async-done | bytes 6291472 | tf_op jit(solution)/shard_map/all_gather | solution.py:36
  231.1 0.0 copy-start.1
  231.1 3.8 convert_reduce_fusion
  234.9 0.7 copy-done.1
  235.7 1.8 fusion.3
  237.5 6.3 %fusion.5 = bf16[512,6144]{1,0:T(8,128)(2,1)} fusion(bf16[512,6144]{1,0:T(8,128)(2,1)S(1)} %copy-done.1, f32[6144]{0:T(1024)S(1)} %bitcast.40, f32[512]{0:T(512)S(1)} %add_rsqrt_fusion, f32[512]{0:T(512)S(1)} %broadcast_multiply_fusion), kind=kLoop, calls=%fused_computation.9 | loop fusion | flops 15728640 | bytes 12611584 | tf_op jit(solution)/shard_map/convert_element_type | solution.py:44
  243.7 50.1 %all-gather.10.cloned.1.call-done = bf16[6144,256]{1,0:T(8,128)(2,1)} async-done(((bf16[192,256]{1,0:T(8,128)(2,1)}), bf16[6144,256]{1,0:T(8,128)(2,1)}) %all-gather.10.cloned.1.call-update) | async-done | bytes 3145744 | tf_op jit(solution)/shard_map/all_gather | solution.py:46
  293.8 5.5 %convolution_convert_fusion.1 = bf16[512,256]{0,1:T(8,128)(2,1)S(1)} fusion(bf16[512,6144]{1,0:T(8,128)(2,1)} %fusion.5, bf16[6144,256]{1,0:T(8,128)(2,1)} %all-gather.10.cloned.1.call-done), kind=kOutput, calls=%fused_computation.15 | convolution fusion | flops 1610743808 | bytes 9699328 | tf_op jit(solution)/shard_map/dot_general | solution.py:51
  299.4 62.3 %all-gather.12.cloned.1.call-done = bf16[6144,256]{1,0:T(8,128)(2,1)} async-done(((bf16[192,256]{1,0:T(8,128)(2,1)}), bf16[6144,256]{1,0:T(8,128)(2,1)}) %all-gather.12.cloned.1.call-update) | async-done | bytes 3145744 | tf_op jit(solution)/shard_map/all_gather | solution.py:47
  361.7 5.5 %convolution_convert_fusion = bf16[512,256]{0,1:T(8,128)(2,1)S(1)} fusion(bf16[512,6144]{1,0:T(8,128)(2,1)} %fusion.5, bf16[6144,256]{1,0:T(8,128)(2,1)} %all-gather.12.cloned.1.call-done), kind=kOutput, calls=%fused_computation.14 | convolution fusion | flops 1610743808 | bytes 9699328 | tf_op jit(solution)/shard_map/dot_general | solution.py:51
  367.2 1.0 fusion.21
  368.2 61.2 %all-gather.8.cloned.1.call-done = bf16[6144,256]{1,0:T(8,128)(2,1)} async-done(((bf16[192,256]{1,0:T(8,128)(2,1)}), bf16[6144,256]{1,0:T(8,128)(2,1)}) %all-gather.8.cloned.1.call-update) | async-done | bytes 3145744 | tf_op jit(solution)/shard_map/all_gather | solution.py:48
  429.4 5.5 %convolution_convert_fusion.2 = bf16[512,256]{0,1:T(8,128)(2,1)S(1)} fusion(bf16[512,6144]{1,0:T(8,128)(2,1)} %fusion.5, bf16[6144,256]{1,0:T(8,128)(2,1)} %all-gather.8.cloned.1.call-done), kind=kOutput, calls=%fused_computation.16 | convolution fusion | flops 1610743808 | bytes 9699328 | tf_op jit(solution)/shard_map/dot_general | solution.py:51
  434.9 1.3 convolution_convert_fusion.3
  436.2 0.8 copy.27
  (11 shorter events, 0.1 us)
Async XLA Ops:
  6.5 1.1 copy-start
  9.4 38.0 %copy-start.2 = (bf16[384]{0:T(512)(128)(2,1)S(1)}, bf16[384]{0:T(512)(128)(2,1)}, u32[]{:S(2)}) copy-start(bf16[384]{0:T(512)(128)(2,1)} %param.8) | copy-start | bytes 2308
  9.4 33.0 %all-to-all-start = ((bf16[32,32,384]{2,1,0:T(8,128)(2,1)}), bf16[32,32,384]{2,1,0:T(8,128)(2,1)S(1)}, u32[]{:S(2)}, u32[]{:S(2)}) async-start(bf16[32,32,384]{2,1,0:T(8,128)(2,1)} %broadcast_select_fusion), calls=%async_computation | async-start | bytes 1572864 | tf_op jit(solution)/shard_map/all_to_all | solution.py:24
  20.0 211.1 %all-gather.6.cloned.1.call-start = ((), (), s32[]{:S(2)}) async-start(), calls=%async_computation.1 | async-start | bytes 6684672 | tf_op jit(solution)/shard_map/all_gather | solution.py:36
  45.3 248.5 %all-gather.10.cloned.1.call-start = ((), (), s32[]{:S(2)}) async-start(), calls=%async_computation.3 | async-start | bytes 3244032 | tf_op jit(solution)/shard_map/all_gather | solution.py:46
  46.1 315.6 %all-gather.12.cloned.1.call-start = ((), (), s32[]{:S(2)}) async-start(), calls=%async_computation.4 | async-start | bytes 3244032 | tf_op jit(solution)/shard_map/all_gather | solution.py:47
  46.8 382.6 %all-gather.8.cloned.1.call-start = ((), (), s32[]{:S(2)}) async-start(), calls=%async_computation.2 | async-start | bytes 3244032 | tf_op jit(solution)/shard_map/all_gather | solution.py:48
  231.1 4.6 %copy-start.1 = (bf16[512,6144]{1,0:T(8,128)(2,1)S(1)}, bf16[512,6144]{1,0:T(8,128)(2,1)}, u32[]{:S(2)}) copy-start(bf16[512,6144]{1,0:T(8,128)(2,1)} %all-gather.6.cloned.1.call-done) | copy-start | bytes 18874372
Sparse Core Ops, SparseCore 0:
  45.5 185.5 all-gather.5
  233.2 60.5 all-gather.9
  296.0 65.6 all-gather.11
  363.7 65.6 all-gather.7
where the time goes:
time: 444 us
  waiting for transfers between devices  329 us (74%)
  blocking collectives  49.9 us (11%)
  matrix products  18.8 us (4%)
  other arithmetic  15.3 us (3%)
  between operations  13.3 us (3%)
  starting transfers between devices  10.7 us (2%)
  local copies, waits for them, and re-layouts  6.03 us (1%)
    all_gather x1, waiting for transfers between devices, shards(): lax.all_gather(packed, 'tensor', axis=1, tiled=True)  133 us
    all_gather x1, waiting for transfers between devices, shards(): lax.all_gather(k_weight, 'dp', axis=0, tiled=True)  62.3 us
    all_gather x1, waiting for transfers between devices, shards(): lax.all_gather(v_weight, 'dp', axis=0, tiled=True)  61.2 us
    all_gather x1, waiting for transfers between devices, shards(): lax.all_gather(q_weight, 'dp', axis=0, tiled=True)  50.1 us
    all_gather x1, blocking collectives, shards(): lax.all_gather(gain, 'tensor', axis=0, tiled=True)  49.9 us
    all_to_all x1, waiting for transfers between devices, shards(): lax.all_to_all(outgoing, 'dp', split_axis=0, concat_axis=0, tiled=True)  20.5 us
    dot_general x3, matrix products, shards(): jnp.dot(normed, weight_rows, preferred_element_type=jnp.float32)  16.6 us
    all_to_all x1, starting transfers between devices, shards(): lax.all_to_all(outgoing, 'dp', split_axis=0, concat_axis=0, tiled=True)  10.6 us
  transfers between devices with their start and end apart: 5, of which 5 were waited for; matrix products, arithmetic and copies ran while one was open for 6% of the time, Pallas kernels for 0%

commit v1 on v0

--- a/solution.py
+++ b/solution.py
@@ -44,7 +44,9 @@
     ).astype(jnp.bfloat16)
     pieces = (
         lax.all_gather(q_weight, "dp", axis=0, tiled=True),
-        lax.all_gather(k_weight, "dp", axis=0, tiled=True),
+        jnp.concatenate(
+            lax.all_to_all(jnp.stack([k_weight] * lax.axis_size("dp")), "dp", 0, 0), axis=0
+        ),
         lax.all_gather(v_weight, "dp", axis=0, tiled=True),
     )
     query_sum, key_sum, value_sum = tuple(

time: 444 us -> 415 us (0.935)
  waiting for transfers between devices: 329 us -> 228 us
  blocking collectives: 49.9 us -> 116 us
  starting transfers between devices: 10.7 us -> 15.5 us
    all_gather x1, waiting for transfers between devices: 133 us -> 61.3 us  [shards(): lax.all_gather(packed, 'tensor', axis=1, tiled=True)]
    all_gather x1, blocking collectives: 49.9 us -> 116 us  [shards(): lax.all_gather(gain, 'tensor', axis=0, tiled=True)]
    all_gather x1 -> x0, waiting for transfers between devices: 62.3 us -> none  [shards(): lax.all_gather(k_weight, 'dp', axis=0, tiled=True)]
    all_gather x1, waiting for transfers between devices: 50.1 us -> 84 us  [shards(): lax.all_gather(q_weight, 'dp', axis=0, tiled=True)]
    all_to_all x0 -> x1, starting transfers between devices: none -> 4.77 us  [shards(): lax.all_to_all(jnp.stack([k_weight] * lax.axis_size('dp')), 'dp', 0, 0)]
  transfers between devices with their start and end apart: 5 -> 5, of which waited for: 5 -> 4; matrix products, arithmetic and copies ran while one was open for 6% -> 7% of each run, Pallas kernels for 0% -> 0%
where the time goes in v1:
time: 415 us
  waiting for transfers between devices  228 us (55%)
  blocking collectives  116 us (28%)
  matrix products  18.8 us (5%)
  starting transfers between devices  15.5 us (4%)
  other arithmetic  15.3 us (4%)
  between operations  13.3 us (3%)
  local copies, waits for them, and re-layouts  8.05 us (2%)
    all_gather x1, blocking collectives, shards(): lax.all_gather(gain, 'tensor', axis=0, tiled=True)  116 us
    all_gather x1, waiting for transfers between devices, shards(): lax.all_gather(q_weight, 'dp', axis=0, tiled=True)  84 us
    all_gather x1, waiting for transfers between devices, shards(): lax.all_gather(v_weight, 'dp', axis=0, tiled=True)  61.3 us
    all_gather x1, waiting for transfers between devices, shards(): lax.all_gather(packed, 'tensor', axis=1, tiled=True)  61.3 us
    all_to_all x1, waiting for transfers between devices, shards(): lax.all_to_all(outgoing, 'dp', split_axis=0, concat_axis=0, tiled=True)  20.5 us
    dot_general x3, matrix products, shards(): jnp.dot(normed, weight_rows, preferred_element_type=jnp.float32)  16.6 us
    all_to_all x1, starting transfers between devices, shards(): lax.all_to_all(outgoing, 'dp', split_axis=0, concat_axis=0, tiled=True)  10.6 us
  transfers between devices with their start and end apart: 5, of which 4 were waited for; matrix products, arithmetic and copies ran while one was open for 7% of the time, Pallas kernels for 0%

profile of v1, /device:TPU:1, one launch (start us, length us, event | category | flops | bytes accessed | tf_op | source)
XLA Modules:
  0.0 415.0 jit_solution(17850209419732960922)
XLA Ops:
  6.5 0.0 copy-start
  6.5 0.8 dynamic-slice_bitcast_fusion
  7.3 0.1 select_reduce_fusion.1
  7.5 0.2 copy-done
  7.7 0.7 gather_fusion
  8.4 1.0 broadcast_select_fusion
  9.4 0.0 copy-start.2
  9.4 10.6 %all-to-all-start = ((bf16[32,32,384]{2,1,0:T(8,128)(2,1)}), bf16[32,32,384]{2,1,0:T(8,128)(2,1)S(1)}, u32[]{:S(2)}, u32[]{:S(2)}) async-start(bf16[32,32,384]{2,1,0:T(8,128)(2,1)} %broadcast_select_fusion), calls=%async_computation | async-start | bytes 1572864 | tf_op jit(solution)/shard_map/all_to_all | solution.py:24
  20.0 0.0 all-gather.5.cloned.1.call-start
  20.1 0.7 fusion.17
  20.8 0.1 copy.23
  20.9 0.1 reduce-window.4
  20.9 0.1 reduce
  21.0 0.1 convert_reduce_fusion.1
  21.1 0.7 fusion.13
  21.8 0.1 select_reduce_fusion
  22.0 20.5 %all-to-all-done = bf16[32,32,384]{2,1,0:T(8,128)(2,1)S(1)} async-done(((bf16[32,32,384]{2,1,0:T(8,128)(2,1)}), bf16[32,32,384]{2,1,0:T(8,128)(2,1)S(1)}, u32[]{:S(2)}, u32[]{:S(2)}) %all-to-all-start) | async-done | bytes 786464 | tf_op jit(solution)/shard_map/all_to_all | solution.py:24
  42.5 1.9 gather_fusion.1
  44.4 0.9 broadcast_select_fusion.1
  45.3 0.0 all-gather.5.cloned.1.call-update
  45.3 0.0 copy-done.2
  45.3 2.0 stack.2
  47.4 0.0 copy-start.3
  47.4 4.8 %all-to-all-start.1 = ((bf16[32,192,256]{2,1,0:T(8,128)(2,1)}), bf16[32,192,256]{2,1,0:T(8,128)(2,1)}, u32[]{:S(2)}, u32[]{:S(2)}) async-start(bf16[32,192,256]{2,1,0:T(8,128)(2,1)} %stack.2), calls=%async_computation.1 | async-start | bytes 6291456 | tf_op jit(solution)/shard_map/all_to_all | solution.py:48
  52.1 0.0 all-gather.9.cloned.1.call-start
  52.2 0.7 all-gather.9.cloned.1.call-update
  52.9 0.0 all-gather.7.cloned.1.call-start
  52.9 0.7 all-gather.7.cloned.1.call-update
  53.6 0.0 copy-done.3
  53.7 115.6 %all-gather = bf16[16,1,384]{2,1,0:T(2,128)(2,1)S(1)} all-gather(bf16[1,1,384]{2,1,0:T(2,128)(2,1)S(1)} %reshape.156), channel_id=1, replica_groups=mesh['dp'=32,'tensor'=16] {'tensor'}, dimensions={0}, use_global_device_ids=true | all-gather | bytes 13056 | tf_op jit(solution)/shard_map/all_gather | solution.py:37
  169.3 0.2 broadcast_compare_fusion
  169.5 61.3 %all-gather.5.cloned.1.call-done = bf16[512,6144]{1,0:T(8,128)(2,1)} async-done(((bf16[512,384]{1,0:T(8,128)(2,1)}), bf16[512,6144]{1,0:T(8,128)(2,1)}) %all-gather.5.cloned.1.call-update) | async-done | bytes 6291472 | tf_op jit(solution)/shard_map/all_gather | solution.py:36
  230.8 0.0 copy-start.1
  230.8 3.8 convert_reduce_fusion
  234.7 0.7 copy-done.1
  235.4 1.8 fusion.3
  237.2 6.3 %fusion.5 = bf16[512,6144]{1,0:T(8,128)(2,1)} fusion(bf16[512,6144]{1,0:T(8,128)(2,1)S(1)} %copy-done.1, f32[6144]{0:T(1024)S(1)} %bitcast.41, f32[512]{0:T(512)S(1)} %add_rsqrt_fusion, f32[512]{0:T(512)S(1)} %broadcast_multiply_fusion), kind=kLoop, calls=%fused_computation.9 | loop fusion | flops 15728640 | bytes 12611584 | tf_op jit(solution)/shard_map/convert_element_type | solution.py:44
  243.5 0.0 all-to-all-done.1
  243.5 5.5 %convolution_convert_fusion = bf16[512,256]{0,1:T(8,128)(2,1)S(1)} fusion(bf16[512,6144]{1,0:T(8,128)(2,1)} %fusion.5, bf16[6144,256]{1,0:T(8,128)(2,1)} %bitcast.13), kind=kOutput, calls=%fused_computation.14 | convolution fusion | flops 1610743808 | bytes 9699328 | tf_op jit(solution)/shard_map/dot_general | solution.py:53
  249.0 84.0 %all-gather.9.cloned.1.call-done = bf16[6144,256]{1,0:T(8,128)(2,1)} async-done(((bf16[192,256]{1,0:T(8,128)(2,1)}), bf16[6144,256]{1,0:T(8,128)(2,1)}) %all-gather.9.cloned.1.call-update) | async-done | bytes 3145744 | tf_op jit(solution)/shard_map/all_gather | solution.py:46
  333.0 5.5 %convolution_convert_fusion.1 = bf16[512,256]{0,1:T(8,128)(2,1)S(1)} fusion(bf16[512,6144]{1,0:T(8,128)(2,1)} %fusion.5, bf16[6144,256]{1,0:T(8,128)(2,1)} %all-gather.9.cloned.1.call-done), kind=kOutput, calls=%fused_computation.15 | convolution fusion | flops 1610743808 | bytes 9699328 | tf_op jit(solution)/shard_map/dot_general | solution.py:53
  338.6 1.0 fusion.21
  339.5 61.3 %all-gather.7.cloned.1.call-done = bf16[6144,256]{1,0:T(8,128)(2,1)} async-done(((bf16[192,256]{1,0:T(8,128)(2,1)}), bf16[6144,256]{1,0:T(8,128)(2,1)}) %all-gather.7.cloned.1.call-update) | async-done | bytes 3145744 | tf_op jit(solution)/shard_map/all_gather | solution.py:50
  400.8 5.5 %convolution_convert_fusion.2 = bf16[512,256]{0,1:T(8,128)(2,1)S(1)} fusion(bf16[512,6144]{1,0:T(8,128)(2,1)} %fusion.5, bf16[6144,256]{1,0:T(8,128)(2,1)} %all-gather.7.cloned.1.call-done), kind=kOutput, calls=%fused_computation.16 | convolution fusion | flops 1610743808 | bytes 9699328 | tf_op jit(solution)/shard_map/dot_general | solution.py:53
  406.4 1.3 convolution_convert_fusion.3
  407.6 0.8 copy.27
  (11 shorter events, 0.1 us)
Async XLA Ops:
  6.5 1.1 copy-start
  9.4 35.9 %copy-start.2 = (bf16[192,256]{1,0:T(8,128)(2,1)S(1)}, bf16[192,256]{1,0:T(8,128)(2,1)}, u32[]{:S(2)}) copy-start(bf16[192,256]{1,0:T(8,128)(2,1)} %param.10) | copy-start | bytes 294916
  9.4 33.0 %all-to-all-start = ((bf16[32,32,384]{2,1,0:T(8,128)(2,1)}), bf16[32,32,384]{2,1,0:T(8,128)(2,1)S(1)}, u32[]{:S(2)}, u32[]{:S(2)}) async-start(bf16[32,32,384]{2,1,0:T(8,128)(2,1)} %broadcast_select_fusion), calls=%async_computation | async-start | bytes 1572864 | tf_op jit(solution)/shard_map/all_to_all | solution.py:24
  20.0 210.8 %all-gather.5.cloned.1.call-start = ((), (), s32[]{:S(2)}) async-start(), calls=%async_computation.2 | async-start | bytes 6684672 | tf_op jit(solution)/shard_map/all_gather | solution.py:36
  47.4 6.3 %copy-start.3 = (bf16[384]{0:T(512)(128)(2,1)S(1)}, bf16[384]{0:T(512)(128)(2,1)}, u32[]{:S(2)}) copy-start(bf16[384]{0:T(512)(128)(2,1)} %param.8) | copy-start | bytes 2308
  47.4 196.1 %all-to-all-start.1 = ((bf16[32,192,256]{2,1,0:T(8,128)(2,1)}), bf16[32,192,256]{2,1,0:T(8,128)(2,1)}, u32[]{:S(2)}, u32[]{:S(2)}) async-start(bf16[32,192,256]{2,1,0:T(8,128)(2,1)} %stack.2), calls=%async_computation.1 | async-start | bytes 6291456 | tf_op jit(solution)/shard_map/all_to_all | solution.py:48
  52.1 280.9 %all-gather.9.cloned.1.call-start = ((), (), s32[]{:S(2)}) async-start(), calls=%async_computation.4 | async-start | bytes 3244032 | tf_op jit(solution)/shard_map/all_gather | solution.py:46
  52.9 347.9 %all-gather.7.cloned.1.call-start = ((), (), s32[]{:S(2)}) async-start(), calls=%async_computation.3 | async-start | bytes 3244032 | tf_op jit(solution)/shard_map/all_gather | solution.py:50
  230.8 4.6 %copy-start.1 = (bf16[512,6144]{1,0:T(8,128)(2,1)S(1)}, bf16[512,6144]{1,0:T(8,128)(2,1)}, u32[]{:S(2)}) copy-start(bf16[512,6144]{1,0:T(8,128)(2,1)} %all-gather.5.cloned.1.call-done) | copy-start | bytes 18874372
Sparse Core Ops, SparseCore 0:
  45.5 185.3 all-gather.4
  233.0 100.0 all-gather.8
  335.2 65.5 all-gather.6
